TPU v7x, 1024 devices: a whole 4x8x16 slice. The times are simulated.
1024 devices in a mesh: ctx: 32 (over y, z_lo), fsdp: 32 (over z_hi, x, core).
Axes of the slice: x: 4, y: 8, z: 16 (z_hi: 4, z_lo: 4; z = z_hi * 4 + z_lo), core: 2. Of those that a mesh axis runs over, the one named last changes fastest.
Arguments:
- grad_out: bfloat16 [4096, 8192], P('ctx', 'fsdp'), may hold values from -6 to 6
- queries: bfloat16 [4096, 8192], P('ctx', 'fsdp'), may hold values from -6 to 6
- keys_in: bfloat16 [4096, 8192], P('ctx', 'fsdp'), may hold values from -6 to 6
- values_in: bfloat16 [4096, 8192], P('ctx', 'fsdp'), may hold values from -6 to 6
- filters: bfloat16 [512, 128], P('fsdp'), may hold values from -1.25 to 1.25
- out_weight: bfloat16 [8192, 8192], P('ctx', 'fsdp'), may hold values from -0.0625 to 0.0625
Outputs:
- grad_q: bfloat16 [4096, 8192], P('ctx', 'fsdp')
- grad_k: bfloat16 [4096, 8192], P('ctx', 'fsdp')
- grad_v: bfloat16 [4096, 8192], P('ctx', 'fsdp')
- grad_filters: float32 [512, 128], P('fsdp')
All inputs are finite; a program needn't handle non-finite values.
Results may differ from a plain program's by a relative error of at most 0.015.
Values may be sent and summed in bfloat16 or wider, within the bound.
A program may use at most 32 MiB of HBM per device.

v0:
```python
import jax
import jax.numpy as jnp
from jax import lax
from jax.sharding import PartitionSpec as P


def from_behind(block, axis, distance):
    devices = range(lax.axis_size(axis))
    route = [(i - distance, i) for i in devices if i - distance in devices]
    return lax.ppermute(block, axis, route)


def toeplitz_rows(line_filters, tokens_here):
    group_count = line_filters.shape[0]
    taps = line_filters.shape[1]
    span = tokens_here + taps - 1
    padded_line = jnp.concatenate(
        [line_filters, jnp.zeros((group_count, span + 1 - taps), line_filters.dtype)], axis=1
    )
    tiled = jnp.tile(padded_line, (1, tokens_here))
    return tiled[:, : tokens_here * span].reshape(group_count, tokens_here, span)


def per_device(grad_out, queries, keys_in, values_in, filters, out_weight):
    tokens_here = grad_out.shape[0]
    channels = grad_out.shape[1]
    group_count = filters.shape[0]
    taps = filters.shape[1]
    per_group = channels // group_count
    margin = taps - 1
    span = tokens_here + margin
    kvp = (keys_in.astype(jnp.float32) * values_in.astype(jnp.float32)).astype(jnp.bfloat16)
    prior = from_behind(kvp[tokens_here - margin :], "ctx", 1)
    kv_ext = jnp.concatenate([prior, kvp], axis=0)
    full_grad = lax.all_gather(grad_out, "fsdp", axis=1, tiled=True)
    grad_y32 = jnp.dot(
        full_grad,
        lax.all_gather(out_weight, "ctx", axis=0, tiled=True),
        preferred_element_type=jnp.float32,
    )
    grad_y = grad_y32.astype(jnp.bfloat16)
    grad_yf = grad_y.astype(jnp.float32)
    forward_toe = toeplitz_rows(filters[:, ::-1], tokens_here)
    kv_groups = kv_ext.reshape(span, group_count, per_group)
    z_conv = jnp.einsum(
        "gts,sgc->tgc", forward_toe, kv_groups, preferred_element_type=jnp.float32
    ).reshape(tokens_here, channels)
    grad_q = (grad_yf * z_conv).astype(jnp.bfloat16)
    grad_z = (grad_yf * queries.astype(jnp.float32)).astype(jnp.bfloat16)
    later = from_behind(grad_z[:margin], "ctx", -1)
    gz_ext = jnp.concatenate([grad_z, later], axis=0)
    backward_toe = toeplitz_rows(filters, tokens_here)
    gz_groups = gz_ext.reshape(span, group_count, per_group)
    grad_kv = jnp.einsum(
        "gts,sgc->tgc", backward_toe, gz_groups, preferred_element_type=jnp.float32
    ).reshape(tokens_here, channels)
    grad_k = (grad_kv * values_in.astype(jnp.float32)).astype(jnp.bfloat16)
    grad_v = (grad_kv * keys_in.astype(jnp.float32)).astype(jnp.bfloat16)
    pairs = jnp.einsum(
        "tgc,sgc->gts",
        grad_z.reshape(tokens_here, group_count, per_group),
        kv_groups,
        preferred_element_type=jnp.float32,
    )
    flat_pairs = pairs.reshape(group_count, tokens_here * span)
    flat_pairs = jnp.concatenate(
        [flat_pairs, jnp.zeros((group_count, tokens_here), jnp.float32)], axis=1
    )
    skewed = flat_pairs.reshape(group_count, tokens_here, span + 1)[:, :, :taps]
    local_terms = jnp.sum(skewed, axis=1)[:, ::-1]
    grad_filters = lax.psum(local_terms, "ctx")
    return (grad_q, grad_k, grad_v, grad_filters)


def solution(mesh):
    placed = (
        P("ctx", "fsdp"),
        P("ctx", "fsdp"),
        P("ctx", "fsdp"),
        P("ctx", "fsdp"),
        P("fsdp", None),
        P("ctx", "fsdp"),
    )
    return jax.shard_map(
        per_device,
        mesh=mesh,
        in_specs=placed,
        out_specs=(P("ctx", "fsdp"), P("ctx", "fsdp"), P("ctx", "fsdp"), P("fsdp", None)),
        check_vma=False,
    )
```

profile of v0, /device:TPU:38, one launch (start us, length us, event | category | flops | bytes accessed | tf_op | source)
XLA Modules:
  0.0 397.8 jit_solution(11727486295466272330)
XLA Ops:
  7.2 0.7 all-gather.3.cloned.1.call-update
  7.9 0.7 all-gather.5.cloned.1.call-update
  8.7 100.4 %all-gather.3.cloned.1.call-done = bf16[128,8192]{1,0:T(8,128)(2,1)} async-done(((bf16[128,256]{1,0:T(8,128)(2,1)}), bf16[128,8192]{1,0:T(8,128)(2,1)}) %all-gather.3.cloned.1.call-update) | async-done | bytes 2097168 | tf_op jit(solution)/shard_map/all_gather | solution.py:35
  109.0 171.6 %all-gather.5.cloned.1.call-done = bf16[8192,256]{1,0:T(8,128)(2,1)} async-done(((bf16[256,256]{1,0:T(8,128)(2,1)}), bf16[8192,256]{1,0:T(8,128)(2,1)}) %all-gather.5.cloned.1.call-update) | async-done | bytes 4194320 | tf_op jit(solution)/shard_map/all_gather | solution.py:38
  280.6 3.6 multiply_convert_fusion
  284.2 5.7 %collective-permute-start.1 = (bf16[127,256]{1,0:T(8,128)(2,1)S(1)}, bf16[127,256]{1,0:T(8,128)(2,1)S(1)}, u32[]{:S(2)}, u32[]{:S(2)}) collective-permute-start(bf16[127,256]{1,0:T(8,128)(2,1)S(1)} %bitcast.32), channel_id=1, source_target_pairs={{32,0},{64,32},{96,64},{128,96},{160,128},{192,160},{224,192},{256... | collective-permute-start | bytes 195080 | tf_op jit(solution)/shard_map/ppermute | solution.py:10
  289.9 0.1 tile.20
  290.0 0.6 copy.23
  290.6 0.1 slice.23
  290.7 3.4 reshape.47
  294.1 0.1 copy.18
  294.2 0.4 fusion.5
  294.6 0.1 copy.19
  294.7 0.7 fusion.1
  295.4 1.9 collective-permute-start
  297.3 0.1 rev.6
  297.4 0.1 tile.8
  297.5 0.6 copy.22
  298.2 3.4 reshape.44
  301.6 0.1 copy.21
  301.7 3.8 collective-permute-done
  305.5 0.1 copy.16
  305.6 0.4 fusion.4
  306.0 0.1 copy.17
  306.1 0.5 fusion.6
  306.6 2.5 reshape.50
  309.1 1.7 concatenate.19
  310.8 0.6 copy.24
  311.4 0.1 slice_reduce_fusion
  311.5 0.1 rev.7
  311.6 78.7 %psum.7 = f32[16,128]{1,0:T(8,128)} all-reduce(f32[16,128]{1,0:T(8,128)S(1)} %rev.7), channel_id=1, replica_groups=mesh['ctx'=32,'fsdp'=32] {'ctx'}, use_global_device_ids=true, to_apply=%region_1.0 | all-reduce | flops 2048 | bytes 16384 | tf_op jit(solution)/shard_map/psum | solution.py:71
  390.3 0.6 multiply_convert_fusion.1
  (15 shorter events, 0.2 us)
Async XLA Ops:
  7.2 101.9 %all-gather.3.cloned.1.call-start = ((), (), s32[]{:S(2)}) async-start(), calls=%async_computation | async-start | bytes 2162688 | tf_op jit(solution)/shard_map/all_gather | solution.py:35
  7.9 272.7 %all-gather.5.cloned.1.call-start = ((), (), s32[]{:S(2)}) async-start(), calls=%async_computation.1 | async-start | bytes 4325376 | tf_op jit(solution)/shard_map/all_gather | solution.py:38
  8.6 281.3 %copy-start.2 = (bf16[16,128]{1,0:T(8,128)(2,1)S(1)}, bf16[16,128]{1,0:T(8,128)(2,1)}, u32[]{:S(2)}) copy-start(bf16[16,128]{1,0:T(8,128)(2,1)} %param.10) | copy-start | bytes 12292
  284.2 9.9 %collective-permute-start.1 = (bf16[127,256]{1,0:T(8,128)(2,1)S(1)}, bf16[127,256]{1,0:T(8,128)(2,1)S(1)}, u32[]{:S(2)}, u32[]{:S(2)}) collective-permute-start(bf16[127,256]{1,0:T(8,128)(2,1)S(1)} %bitcast.32), channel_id=1, source_target_pairs={{32,0},{64,32},{96,64},{128,96},{160,128},{192,160},{224,192},{256... | collective-permute-start | bytes 195080 | tf_op jit(solution)/shard_map/ppermute | solution.py:10
  290.7 4.0 %copy-start = (bf16[128,256]{1,0:T(8,128)(2,1)S(1)}, bf16[128,256]{1,0:T(8,128)(2,1)}, u32[]{:S(2)}) copy-start(bf16[128,256]{1,0:T(8,128)(2,1)} %param.8) | copy-start | bytes 196612
  290.7 4.0 %copy-start.1 = (bf16[128,256]{1,0:T(8,128)(2,1)S(1)}, bf16[128,256]{1,0:T(8,128)(2,1)}, u32[]{:S(2)}) copy-start(bf16[128,256]{1,0:T(8,128)(2,1)} %param.9) | copy-start | bytes 196612
  295.4 10.1 %collective-permute-start = (bf16[127,256]{1,0:T(8,128)(2,1)S(1)}, bf16[127,256]{1,0:T(8,128)(2,1)S(1)}, u32[]{:S(2)}, u32[]{:S(2)}) collective-permute-start(bf16[127,256]{1,0:T(8,128)(2,1)S(1)} %slice.20), channel_id=1, source_target_pairs={{0,32},{32,64},{64,96},{96,128},{128,160},{160,192},{192,224},{224... | collective-permute-start | bytes 195080 | tf_op jit(solution)/shard_map/ppermute | solution.py:10
Sparse Core Ops, SparseCore 0:
  12.2 96.7 all-gather.2
  111.7 168.8 all-gather.4
where the time goes:
time: 398 us
  waiting for transfers between devices  277 us (70%)
  blocking collectives  78.7 us (20%)
  between operations  14.3 us (4%)
  local copies, waits for them, and re-layouts  13.8 us (3%)
  starting transfers between devices  7.68 us (2%)
  matrix products  4.78 us (1%)
    all_gather x1, waiting for transfers between devices, per_device(): lax.all_gather(out_weight, 'ctx', axis=0, tiled=True)  172 us
    all_gather x1, waiting for transfers between devices, per_device(): full_grad = lax.all_gather(grad_out, 'fsdp', axis=1, tiled=True)  100 us
    psum x1, blocking collectives, per_device(): grad_filters = lax.psum(local_terms, 'ctx')  78.7 us
  transfers between devices with their start and end apart: 4, of which 3 were waited for; matrix products, arithmetic and copies ran while one was open for 2% of the time, Pallas kernels for 0%

commit v1 on v0

v1 whole, which is shorter than its diff:
```python
import jax
import jax.numpy as jnp
from jax import lax
from jax.experimental import pallas as pl
from jax.experimental.pallas import tpu as pltpu
from jax.sharding import PartitionSpec as P

MESH = pl.DeviceIdType.MESH
NX, NY, NH, NL = 4, 8, 4, 4
NZ = NH * NL
ROWS = 128
WIDE = 256
HALF = 64
GROUPS = 16
TAPS = 128
F32, BF16 = jnp.float32, jnp.bfloat16


def mod(value, size):
    return lax.rem(value + size, size)


def kernel(
    go, queries, keys, values, filters, weight,
    out_q, out_k, out_v, out_f,
    grads, rows_w, staged, part, part_in, kvx, kvrev, gzx, toe_z, toe_b, conv, sums_l, sums_y,
    w_send, w_recv, pre_send, pre_recv, z1_send, z2_send, z_recv, x_send, x_recv, sib_send, sib_recv,
    halo_send, halo_recv, part_send, part_recv, l_send, l_recv, y_send, y_recv,
):
    ctx = lax.axis_index("ctx")
    fsdp = lax.axis_index("fsdp")
    y, l = lax.div(ctx, NL), lax.rem(ctx, NL)
    h, x, k = lax.div(fsdp, NX * 2), lax.rem(lax.div(fsdp, 2), NX), lax.rem(fsdp, 2)
    z = h * NL + l
    side = 1 - 2 * k

    def device(x_=None, y_=None, z_=None, k_=None):
        x_, y_ = (x if x_ is None else x_), (y if y_ is None else y_)
        z_, k_ = (z if z_ is None else z_), (k if k_ is None else k_)
        h_, l_ = lax.div(z_, NL), lax.rem(z_, NL)
        return (y_ * NL + l_, h_ * (NX * 2) + x_ * 2 + k_)

    def along(step):
        other = mod(ctx + step, NY * NL)
        return (other, fsdp)

    def remote(src, dst, send, recv, target):
        return pltpu.make_async_remote_copy(
            src_ref=src, dst_ref=dst, send_sem=send, recv_sem=recv, device_id=target, device_id_type=MESH
        )

    is_home = k == lax.rem(l, 2)

    barrier = pltpu.get_barrier_semaphore()

    def greet(target):
        pl.semaphore_signal(barrier, inc=1, device_id=target, device_id_type=MESH)

    near_x = (mod(x - 1, NX), mod(x + 1, NX))
    near_y = (mod(y - 1, NY), mod(y + 1, NY))
    for other in near_y:
        greet(device(y_=other))
    greet(device(x_=near_x[0]))
    for j in range(1, 5):
        greet(device(z_=mod(z - side * j, NZ), k_=lax.rem(l, 2)))
    greet(device(z_=mod(z - side * 4, NZ)))
    for other in near_x:
        greet(device(x_=other))
    greet(device(k_=1 - k))
    for i in range(1, NL):
        greet(device(z_=h * NL + mod(l + i, NL)))
    for i in range(1, NY):
        greet(device(y_=mod(y + i, NY)))
    greet(along(1))
    greet(along(-1))

    kvp = (keys[...].astype(F32) * values[...].astype(F32)).astype(BF16)
    kvx[ROWS:, :] = kvp
    rows_w[pl.ds(y, 1)] = weight[...].reshape(1, WIDE, WIDE)

    lane = lax.broadcasted_iota(jnp.int32, (TAPS, WIDE), 1)
    row = lax.broadcasted_iota(jnp.int32, (TAPS, WIDE), 0)
    plain = jnp.dot(filters[...], (lane == row).astype(BF16), preferred_element_type=F32)
    turned = jnp.dot(filters[...], (lane == TAPS - row).astype(BF16), preferred_element_type=F32)
    conv[0:GROUPS, :] = plain
    conv[GROUPS : 2 * GROUPS, :] = turned

    def build(g, _):
        line_b = jnp.broadcast_to(conv[pl.ds(g, 1), :], (ROWS, WIDE))
        line_z = jnp.broadcast_to(conv[pl.ds(GROUPS + g, 1), :], (ROWS, WIDE))
        toe_b[g] = pltpu.roll(line_b, 0, 1, stride=1, stride_axis=0).astype(BF16)
        toe_z[g] = pltpu.roll(line_z, 0, 1, stride=1, stride_axis=0).astype(BF16)
        return 0

    lax.fori_loop(0, GROUPS, build, 0)

    pl.semaphore_wait(barrier, 2 + 1 + 4 + 1 + 2 + 1 + (NL - 1) + (NY - 1) + 2)

    started = []

    def go_now(copy):
        copy.start()
        started.append(copy)

    def w_copy(direction, step, sub):
        owner = mod(y - step, NY) if direction == 0 else mod(y + step, NY)
        block = rows_w.at[owner, pl.ds(sub * ROWS, ROWS), :]
        return remote(
            block, block, w_send.at[direction, step, sub], w_recv.at[direction, step, sub],
            device(y_=near_y[1 - direction]),
        )

    def w_arrived(direction, step, sub):
        owner = mod(y - step, NY) if direction == 0 else mod(y + step, NY)
        block = rows_w.at[owner, pl.ds(sub * ROWS, ROWS), :]
        remote(
            block, block, w_send.at[direction, step - 1, sub], w_recv.at[direction, step - 1, sub],
            device(y_=near_y[1 - direction]),
        ).wait_recv()

    def piece(xs, k_, j, l_dest=None):
        l_dest = l if l_dest is None else l_dest
        z_from = mod(z - (1 - 2 * k_) * j, NZ)
        p = lax.rem(xs + 4 - lax.div(l_dest, 2), 2)
        x_from = mod(xs - p, NX)
        feature = 2 * lax.div(z_from, NL) + lax.div(x_from, 2)
        first = lax.rem(z_from, NL) * ROWS + p * HALF
        if j == 8:
            return grads.at[feature, pl.ds(pl.multiple_of(first + k_ * 32, 32), 32), :]
        return grads.at[feature, pl.ds(pl.multiple_of(first, HALF), HALF), :]

    def first_hop(p):
        src = go.at[pl.ds(0, HALF), :] if p == 0 else staged
        x_from = x if p == 0 else near_x[0]
        l_dest = 2 * lax.rem(x_from, 2) + k
        apart = mod(l_dest - l, NL)
        dst = grads.at[
            2 * h + lax.div(x_from, 2), pl.ds(pl.multiple_of(l * ROWS + p * HALF, HALF), HALF), :
        ]
        right = jnp.where(apart == 0, 4, apart)
        left = 4 - apart
        go_now(remote(src, dst, z1_send.at[p, 0], z_recv.at[right],
                      device(z_=mod(z + right, NZ), k_=0)))
        go_now(remote(src, dst, z1_send.at[p, 1], z_recv.at[left],
                      device(z_=mod(z - left, NZ), k_=1)))

    go_now(remote(go.at[pl.ds(HALF, HALF), :], staged, pre_send, pre_recv, device(x_=near_x[1])))
    first_hop(0)
    for sub in range(2):
        go_now(w_copy(0, 0, sub))
        go_now(w_copy(1, 0, 1 - sub))
    go_now(remote(kvx.at[pl.ds(ROWS, ROWS), :], kvx.at[pl.ds(0, ROWS), :],
                  halo_send.at[0], halo_recv.at[0], along(1)))
    remote(go.at[pl.ds(HALF, HALF), :], staged, pre_send, pre_recv, device(x_=near_x[1])).wait_recv()
    first_hop(1)

    def own_out(j):
        block = piece(x, k, j)
        return [
            remote(block, block, sib_send.at[0, j], sib_recv.at[0, j], device(k_=1 - k)),
            remote(block, block, x_send.at[0, j], x_recv.at[0, j], device(x_=near_x[1])),
            remote(block, block, x_send.at[1, j], x_recv.at[1, j], device(x_=near_x[0])),
        ]

    def own_event(j):
        block = piece(x, k, j)
        remote(block, block, z2_send.at[0], z_recv.at[j], device(k_=1 - k)).wait_recv()
        if j <= 4:
            farther = mod(z + side * 4, NZ)
            src = block
            if j == 4:
                z_from = mod(z - side * j, NZ)
                p = lax.rem(x + 4 - lax.div(l, 2), 2)
                feature = 2 * lax.div(z_from, NL) + lax.div(mod(x - p, NX), 2)
                first = lax.rem(z_from, NL) * ROWS + p * HALF + k * 32
                src = grads.at[feature, pl.ds(pl.multiple_of(first, 32), 32), :]
            go_now(remote(src, src, z2_send.at[j], z_recv.at[j + 4], device(z_=farther)))
        for copy in own_out(j):
            go_now(copy)

    def side_stream(index):
        return near_x[0] if index == 0 else near_x[1]

    first_x = jnp.where(k == 0, near_x[0], near_x[1])
    second_x = jnp.where(k == 0, near_x[1], near_x[0])
    onward = second_x
    across = mod(x + 2, NX)

    def first_out(j):
        block = piece(first_x, k, j)
        return [
            remote(block, block, x_send.at[2, j], x_recv.at[2, j], device(x_=onward)),
            remote(block, block, sib_send.at[1, j], sib_recv.at[1, j], device(k_=1 - k)),
        ]

    def second_out(j):
        block = piece(second_x, k, j)
        return [remote(block, block, sib_send.at[2, j], sib_recv.at[2, j], device(k_=1 - k))]

    def across_out(j):
        block = piece(across, k, j)
        return [remote(block, block, sib_send.at[3, j], sib_recv.at[3, j], device(k_=1 - k))]

    def arrived(block, slot, j):
        remote(block, block, x_send.at[0, j], x_recv.at[slot, j], device(k_=1 - k)).wait_recv()

    def side_event(j):
        arrived(piece(first_x, k, j), k, j)
        for copy in first_out(j):
            go_now(copy)
        arrived(piece(second_x, k, j), 1 - k, j)
        for copy in second_out(j):
            go_now(copy)

    def across_event(j):
        arrived(piece(across, k, j), 2, j)
        for copy in across_out(j):
            go_now(copy)

    def w_event(step, i):
        for direction in range(2):
            sub = i if direction == 0 else 1 - i
            w_arrived(direction, step, sub)
            if step < 3 or (step == 3 and i == 0):
                go_now(w_copy(direction, step, sub))

    @pl.when(is_home)
    def _():
        p = lax.rem(x + 4 - lax.div(l, 2), 2)
        block = piece(x, k, 0)
        block[...] = jnp.where(p == 0, go[0:HALF, :], staged[...])
        for copy in own_out(0):
            copy.start()

    def home_side():
        @pl.when(is_home)
        def _():
            arrived(piece(first_x, k, 0), k, 0)
            for copy in first_out(0):
                copy.start()
            arrived(piece(second_x, k, 0), 1 - k, 0)
            for copy in second_out(0):
                copy.start()

    def home_across():
        @pl.when(is_home)
        def _():
            arrived(piece(across, k, 0), 2, 0)
            for copy in across_out(0):
                copy.start()

    own_event(1)
    own_event(2)
    w_event(1, 0)
    own_event(3)
    home_side()
    w_event(1, 1)
    own_event(4)
    side_event(1)
    home_across()
    side_event(2)
    w_event(2, 0)
    own_event(5)
    side_event(3)
    across_event(1)
    w_event(2, 1)
    own_event(6)
    side_event(4)
    across_event(2)
    own_event(7)
    w_event(3, 0)
    side_event(5)
    across_event(3)
    own_event(8)
    w_event(3, 1)
    side_event(6)
    across_event(4)
    side_event(7)
    across_event(5)
    side_event(8)
    for j in (6, 7, 8):
        across_event(j)
    w_arrived(0, 4, 0)
    w_arrived(1, 4, 1)

    def from_sibling(stream, xs, j):
        block = piece(xs, 1 - k, j)
        remote(block, block, sib_send.at[stream, j], sib_recv.at[stream, j], device(k_=1 - k)).wait_recv()

    streams = ((0, x), (1, second_x), (2, first_x), (3, across))
    for j in range(1, 9):
        for stream, xs in streams:
            from_sibling(stream, xs, j)

    @pl.when(jnp.logical_not(is_home))
    def _():
        for stream, xs in streams:
            from_sibling(stream, xs, 0)

    def partial(tl):
        rows = pl.ds(pl.multiple_of(tl * ROWS, ROWS), ROWS)
        left = jnp.concatenate([grads[i, rows, :] for i in range(NY)], axis=1)
        right = rows_w[...].reshape(NY * WIDE, WIDE)
        return jnp.dot(left, right, preferred_element_type=F32)

    def part_copy(i):
        return remote(part.at[i - 1], part_in.at[i - 1], part_send.at[i - 1], part_recv.at[i - 1],
                      device(z_=h * NL + mod(l + i, NL)))

    for i in (2, 1, 3):
        part[i - 1] = partial(mod(l + i, NL)).astype(BF16)
        go_now(part_copy(i))
    mine = partial(l)

    remote(kvx.at[pl.ds(ROWS, ROWS), :], kvx.at[pl.ds(0, ROWS), :],
           halo_send.at[0], halo_recv.at[0], along(1)).wait_recv()
    kvx[0:ROWS, :] = jnp.where(ctx > 0, kvx[0:ROWS, :], jnp.zeros((ROWS, WIDE), BF16))
    group_of = lax.div(lax.broadcasted_iota(jnp.int32, (ROWS, WIDE), 1), WIDE // GROUPS)

    def forward(g, total):
        term = jnp.dot(toe_z[g], kvx[...], preferred_element_type=F32)
        return jnp.where(group_of == g, term, total)

    zeros = jnp.zeros((ROWS, WIDE), F32)
    conv[...] = lax.fori_loop(0, GROUPS, forward, zeros)
    flip = (
        lax.broadcasted_iota(jnp.int32, (WIDE, WIDE), 0) + lax.broadcasted_iota(jnp.int32, (WIDE, WIDE), 1)
        == WIDE - 1
    ).astype(BF16)
    kvrev[0:WIDE, :] = jnp.dot(flip, kvx[...], preferred_element_type=F32).astype(BF16)
    kvrev[WIDE:, :] = jnp.zeros((ROWS, WIDE), BF16)

    total = mine
    for i in (1, 2, 3):
        part_copy(i).wait_recv()
        total = total + part_in[i - 1].astype(F32)
    grad_y = total.astype(BF16).astype(F32)
    grad_z = (grad_y * queries[...].astype(F32)).astype(BF16)
    gzx[0:ROWS, :] = grad_z

    def later():
        return remote(gzx.at[pl.ds(0, ROWS), :], gzx.at[pl.ds(ROWS, ROWS), :],
                      halo_send.at[1], halo_recv.at[1], along(-1))

    go_now(later())
    out_q[...] = (grad_y * conv[...]).astype(BF16)

    keep = lax.div(lax.broadcasted_iota(jnp.int32, (WIDE, WIDE), 0), 16) == lax.div(
        lax.broadcasted_iota(jnp.int32, (WIDE, WIDE), 1), WIDE // GROUPS
    )
    cross = jnp.zeros((WIDE, WIDE), F32)
    for a in range(8):
        tokens = gzx[16 * a : 16 * a + 16, :]
        left = jnp.where(keep, jnp.concatenate([tokens] * GROUPS, axis=0), jnp.zeros((WIDE, WIDE), BF16))
        right = kvrev[112 - 16 * a : 112 - 16 * a + WIDE, :]
        cross = cross + lax.dot_general(left, right, (((1,), (1,)), ((), ())), preferred_element_type=F32)
    lines = []
    for g in range(GROUPS):
        turned_g = pltpu.roll(cross[16 * g : 16 * g + 16, :], WIDE - 15, 1, stride=1, stride_axis=0)
        lines.append(jnp.sum(turned_g, axis=0, keepdims=True)[:, 0:TAPS])
    sums_l[pl.ds(l, 1)] = jnp.concatenate(lines, axis=0).reshape(1, GROUPS, TAPS)

    def l_copy(i, slot):
        return remote(sums_l.at[slot], sums_l.at[slot], l_send.at[i - 1], l_recv.at[i - 1],
                      device(z_=h * NL + mod(l + i, NL)))

    def y_copy(i, slot):
        return remote(sums_y.at[slot], sums_y.at[slot], y_send.at[i - 1], y_recv.at[i - 1],
                      device(y_=mod(y + i, NY)))

    for i in range(1, NL):
        go_now(l_copy(i, l))

    def back_here(g, total_):
        term = jnp.dot(toe_b[g, :, 0:ROWS], gzx[0:ROWS, :], preferred_element_type=F32)
        return jnp.where(group_of == g, term, total_)

    conv[...] = lax.fori_loop(0, GROUPS, back_here, zeros)

    for i in range(1, NL):
        l_copy(i, mod(l - i, NL)).wait_recv()
    sums_y[pl.ds(y, 1)] = (((sums_l[0] + sums_l[1]) + sums_l[2]) + sums_l[3]).reshape(1, GROUPS, TAPS)
    for i in range(1, NY):
        go_now(y_copy(i, y))

    later().wait_recv()
    gzx[ROWS:, :] = jnp.where(ctx < NY * NL - 1, gzx[ROWS:, :], jnp.zeros((ROWS, WIDE), BF16))

    def back_later(g, total_):
        term = jnp.dot(toe_b[g, :, ROWS:], gzx[ROWS:, :], preferred_element_type=F32)
        return jnp.where(group_of == g, term, total_)

    grad_kv = conv[...] + lax.fori_loop(0, GROUPS, back_later, zeros)
    out_k[...] = (grad_kv * values[...].astype(F32)).astype(BF16)
    out_v[...] = (grad_kv * keys[...].astype(F32)).astype(BF16)

    for copy in started:
        copy.wait_send()

    @pl.when(is_home)
    def _():
        for copy in own_out(0) + first_out(0) + second_out(0) + across_out(0):
            copy.wait_send()

    for i in range(1, NY):
        y_copy(i, mod(y - i, NY)).wait_recv()
    final = sums_y[0]
    for i in range(1, NY):
        final = final + sums_y[i]
    out_f[...] = final


def per_device(*arrays):
    vmem = pl.BlockSpec(memory_space=pltpu.VMEM)
    dma = pltpu.SemaphoreType.DMA
    return pl.pallas_call(
        kernel,
        out_shape=(
            jax.ShapeDtypeStruct((ROWS, WIDE), BF16),
            jax.ShapeDtypeStruct((ROWS, WIDE), BF16),
            jax.ShapeDtypeStruct((ROWS, WIDE), BF16),
            jax.ShapeDtypeStruct((GROUPS, TAPS), F32),
        ),
        in_specs=[vmem] * 6,
        out_specs=(vmem,) * 4,
        scratch_shapes=[
            pltpu.VMEM((NY, NL * ROWS, WIDE), BF16),
            pltpu.VMEM((NY, WIDE, WIDE), BF16),
            pltpu.VMEM((HALF, WIDE), BF16),
            pltpu.VMEM((NL - 1, ROWS, WIDE), BF16),
            pltpu.VMEM((NL - 1, ROWS, WIDE), BF16),
            pltpu.VMEM((2 * ROWS, WIDE), BF16),
            pltpu.VMEM((3 * ROWS, WIDE), BF16),
            pltpu.VMEM((2 * ROWS, WIDE), BF16),
            pltpu.VMEM((GROUPS, ROWS, WIDE), BF16),
            pltpu.VMEM((GROUPS, ROWS, WIDE), BF16),
            pltpu.VMEM((ROWS, WIDE), F32),
            pltpu.VMEM((NL, GROUPS, TAPS), F32),
            pltpu.VMEM((NY, GROUPS, TAPS), F32),
            dma((2, 4, 2)), dma((2, 4, 2)), dma, dma, dma((2, 2)), dma((5,)), dma((9,)),
            dma((3, 9)), dma((3, 9)), dma((4, 9)), dma((4, 9)),
            dma((2,)), dma((2,)), dma((NL - 1,)), dma((NL - 1,)),
            dma((NL - 1,)), dma((NL - 1,)), dma((NY - 1,)), dma((NY - 1,)),
        ],
        compiler_params=pltpu.CompilerParams(collective_id=0, has_side_effects=True),
        name="block_backward",
    )(*arrays)


def solution(mesh):
    here = P("ctx", "fsdp")
    return jax.shard_map(
        per_device,
        mesh=mesh,
        in_specs=(here, here, here, here, P("fsdp", None), here),
        out_specs=(here, here, here, P("fsdp", None)),
        check_vma=False,
    )
```

time: 398 us -> 71.5 us (0.18)
  the two profiles are of different devices: /device:TPU:38 before, /device:TPU:1 now
where the time goes in v1:
time: 71.5 us; the launch traced here: 71.2 us
  Pallas kernels  66.9 us (94%)
  local copies, waits for them, and re-layouts  3.66 us (5%)
    pallas_call x1, Pallas kernels, per_device(): pl.pallas_call(kernel, out_shape=(jax.ShapeDtypeStruct((ROWS, WIDE), BF16...  66.9 us
    unnamed x10, local copies, waits for them, and re-layouts  3.66 us

profile of v1, /device:TPU:1, one launch (start us, length us, event | category | flops | bytes accessed | tf_op | source)
XLA Modules:
  0.0 71.2 jit_solution(13831888030388723871)
XLA Ops:
  0.6 66.9 %block_backward.1 = (bf16[128,256]{1,0:T(8,128)(2,1)}, bf16[128,256]{1,0:T(8,128)(2,1)}, bf16[128,256]{1,0:T(8,128)(2,1)}, f32[16,128]{1,0:T(8,128)}) custom-call(bf16[128,256]{1,0:T(8,128)(2,1)} %go.1, bf16[128,256]{1,0:T(8,128)(2,1)} %queries.1, bf16[128,256]{1,0:T(8,128)(2,1)} %keys.1, bf16[128,256]{1,0:T(8,128)(2,1)} %values.1, bf16[16,128]{1,0:T(8,128)(2,1)} %filters.1, ...), custom_call_target="tpu_custom_call" | custom-call | tf_op jit(solution)/shard_map/block_backward/pallas_call | solution.py:416
  67.5 0.0 copy-start.1
  67.5 1.5 %copy.14 = bf16[128,256]{1,0:T(8,128)(2,1)} copy(bf16[128,256]{1,0:T(8,128)(2,1)} %get-tuple-element.8) | data formatting | bytes 131072
  69.0 0.0 copy-done.1
  69.0 0.0 copy-start
  69.0 0.6 copy.15
  69.7 0.2 copy-done
  69.9 0.0 copy-start.2
  69.9 0.6 copy.16
  70.5 0.1 copy-done.2
  70.6 0.6 copy.17
Async XLA Ops:
  67.5 1.5 %copy-start.1 = (bf16[128,256]{1,0:T(8,128)(2,1)S(1)}, bf16[128,256]{1,0:T(8,128)(2,1)}, u32[]{:S(2)}) copy-start(bf16[128,256]{1,0:T(8,128)(2,1)} %get-tuple-element.9) | copy-start | bytes 196612
  69.0 0.9 %copy-start = (bf16[128,256]{1,0:T(8,128)(2,1)S(1)}, bf16[128,256]{1,0:T(8,128)(2,1)}, u32[]{:S(2)}) copy-start(bf16[128,256]{1,0:T(8,128)(2,1)} %get-tuple-element.10) | copy-start | bytes 196612
  69.9 0.7 copy-start.2

commit v2 on v1

--- a/solution.py
+++ b/solution.py
@@ -21,9 +21,10 @@
 
 
 def kernel(
-    go, queries, keys, values, filters, weight,
+    go_in, queries_in, keys_in, values_in, filters_in, weight_in,
     out_q, out_k, out_v, out_f,
-    grads, rows_w, staged, part, part_in, kvx, kvrev, gzx, toe_z, toe_b, conv, sums_l, sums_y,
+    go, queries, keys, values, filters, load_sem, hello_y,
+    grads, rows_w, part, part_in, kvx, kvrev, gzx, toe_z, toe_b, conv, sums_l, sums_y,
     w_send, w_recv, pre_send, pre_recv, z1_send, z2_send, z_recv, x_send, x_recv, sib_send, sib_recv,
     halo_send, halo_recv, part_send, part_recv, l_send, l_recv, y_send, y_recv,
 ):
@@ -58,43 +59,30 @@
 
     near_x = (mod(x - 1, NX), mod(x + 1, NX))
     near_y = (mod(y - 1, NY), mod(y + 1, NY))
+    p_here = lax.rem(x + 4 - lax.div(l, 2), 2)
     for other in near_y:
         greet(device(y_=other))
-    greet(device(x_=near_x[0]))
-    for j in range(1, 5):
-        greet(device(z_=mod(z - side * j, NZ), k_=lax.rem(l, 2)))
-    greet(device(z_=mod(z - side * 4, NZ)))
     for other in near_x:
         greet(device(x_=other))
     greet(device(k_=1 - k))
+    for j in range(1, 5):
+        greet(device(x_=mod(x - p_here, NX), z_=mod(z - side * j, NZ), k_=lax.rem(l, 2)))
+    greet(device(z_=mod(z - side * 4, NZ)))
     for i in range(1, NL):
         greet(device(z_=h * NL + mod(l + i, NL)))
-    for i in range(1, NY):
-        greet(device(y_=mod(y + i, NY)))
-    greet(along(1))
-    greet(along(-1))
-
-    kvp = (keys[...].astype(F32) * values[...].astype(F32)).astype(BF16)
-    kvx[ROWS:, :] = kvp
-    rows_w[pl.ds(y, 1)] = weight[...].reshape(1, WIDE, WIDE)
-
-    lane = lax.broadcasted_iota(jnp.int32, (TAPS, WIDE), 1)
-    row = lax.broadcasted_iota(jnp.int32, (TAPS, WIDE), 0)
-    plain = jnp.dot(filters[...], (lane == row).astype(BF16), preferred_element_type=F32)
-    turned = jnp.dot(filters[...], (lane == TAPS - row).astype(BF16), preferred_element_type=F32)
-    conv[0:GROUPS, :] = plain
-    conv[GROUPS : 2 * GROUPS, :] = turned
-
-    def build(g, _):
-        line_b = jnp.broadcast_to(conv[pl.ds(g, 1), :], (ROWS, WIDE))
-        line_z = jnp.broadcast_to(conv[pl.ds(GROUPS + g, 1), :], (ROWS, WIDE))
-        toe_b[g] = pltpu.roll(line_b, 0, 1, stride=1, stride_axis=0).astype(BF16)
-        toe_z[g] = pltpu.roll(line_z, 0, 1, stride=1, stride_axis=0).astype(BF16)
-        return 0
-
-    lax.fori_loop(0, GROUPS, build, 0)
-
-    pl.semaphore_wait(barrier, 2 + 1 + 4 + 1 + 2 + 1 + (NL - 1) + (NY - 1) + 2)
+
+    loads = [
+        pltpu.make_async_copy(src, dst, load_sem.at[i])
+        for i, (src, dst) in enumerate((
+            (go_in, go), (weight_in, rows_w.at[y]), (keys_in, keys), (values_in, values),
+            (filters_in, filters), (queries_in, queries),
+        ))
+    ]
+    for load in loads:
+        load.start()
+    loads[0].wait()
+    loads[1].wait()
+    pl.semaphore_wait(barrier, 2 + 2 + 1 + 4 + 1 + (NL - 1))
 
     started = []
 
@@ -129,30 +117,60 @@
             return grads.at[feature, pl.ds(pl.multiple_of(first + k_ * 32, 32), 32), :]
         return grads.at[feature, pl.ds(pl.multiple_of(first, HALF), HALF), :]
 
-    def first_hop(p):
-        src = go.at[pl.ds(0, HALF), :] if p == 0 else staged
-        x_from = x if p == 0 else near_x[0]
-        l_dest = 2 * lax.rem(x_from, 2) + k
-        apart = mod(l_dest - l, NL)
+    def first_hop(p, direction):
+        apart = mod(2 * lax.rem(x, 2) + k - l, NL)
+        steps = jnp.where(apart == 0, 4, apart) if direction == 0 else 4 - apart
+        target = mod(z + steps, NZ) if direction == 0 else mod(z - steps, NZ)
         dst = grads.at[
-            2 * h + lax.div(x_from, 2), pl.ds(pl.multiple_of(l * ROWS + p * HALF, HALF), HALF), :
+            2 * h + lax.div(x, 2), pl.ds(pl.multiple_of(l * ROWS + p * HALF, HALF), HALF), :
         ]
-        right = jnp.where(apart == 0, 4, apart)
-        left = 4 - apart
-        go_now(remote(src, dst, z1_send.at[p, 0], z_recv.at[right],
-                      device(z_=mod(z + right, NZ), k_=0)))
-        go_now(remote(src, dst, z1_send.at[p, 1], z_recv.at[left],
-                      device(z_=mod(z - left, NZ), k_=1)))
-
-    go_now(remote(go.at[pl.ds(HALF, HALF), :], staged, pre_send, pre_recv, device(x_=near_x[1])))
-    first_hop(0)
+        return remote(go.at[pl.ds(p * HALF, HALF), :], dst, z1_send.at[p, direction], z_recv.at[steps],
+                      device(x_=x if p == 0 else near_x[1], z_=target, k_=direction))
+
+    home_half = 2 * lax.rem(x, 2) + k == l
+
+    def pre_copy():
+        dst = grads.at[
+            2 * h + lax.div(x, 2), pl.ds(pl.multiple_of(l * ROWS + HALF, HALF), HALF), :
+        ]
+        return remote(go.at[pl.ds(HALF, HALF), :], dst, pre_send, pre_recv, device(x_=near_x[1]))
+
+    @pl.when(home_half)
+    def _():
+        pre_copy().start()
+
+    for p in range(2):
+        for direction in range(2):
+            go_now(first_hop(p, direction))
     for sub in range(2):
         go_now(w_copy(0, 0, sub))
         go_now(w_copy(1, 0, 1 - sub))
-    go_now(remote(kvx.at[pl.ds(ROWS, ROWS), :], kvx.at[pl.ds(0, ROWS), :],
-                  halo_send.at[0], halo_recv.at[0], along(1)))
-    remote(go.at[pl.ds(HALF, HALF), :], staged, pre_send, pre_recv, device(x_=near_x[1])).wait_recv()
-    first_hop(1)
+
+    @pl.when(l == NL - 1)
+    def _():
+        pl.semaphore_signal(hello_y, inc=1, device_id=device(y_=near_y[0]), device_id_type=MESH)
+
+    for load in loads[2:]:
+        load.wait()
+    kvp = (keys[...].astype(F32) * values[...].astype(F32)).astype(BF16)
+    kvx[ROWS:, :] = kvp
+
+    lane = lax.broadcasted_iota(jnp.int32, (TAPS, WIDE), 1)
+    row = lax.broadcasted_iota(jnp.int32, (TAPS, WIDE), 0)
+    plain = jnp.dot(filters[...], (lane == row).astype(BF16), preferred_element_type=F32)
+    turned = jnp.dot(filters[...], (lane == TAPS - row).astype(BF16), preferred_element_type=F32)
+    conv[0:GROUPS, :] = plain
+    conv[GROUPS : 2 * GROUPS, :] = turned
+
+    def build(g, _):
+        line_b = jnp.broadcast_to(conv[pl.ds(g, 1), :], (ROWS, WIDE))
+        line_z = jnp.broadcast_to(conv[pl.ds(GROUPS + g, 1), :], (ROWS, WIDE))
+        toe_b[g] = pltpu.roll(line_b, 0, 1, stride=1, stride_axis=0).astype(BF16)
+        toe_z[g] = pltpu.roll(line_z, 0, 1, stride=1, stride_axis=0).astype(BF16)
+        return 0
+
+    lax.fori_loop(0, GROUPS, build, 0)
+
 
     def own_out(j):
         block = piece(x, k, j)
@@ -170,32 +188,22 @@
             src = block
             if j == 4:
                 z_from = mod(z - side * j, NZ)
-                p = lax.rem(x + 4 - lax.div(l, 2), 2)
-                feature = 2 * lax.div(z_from, NL) + lax.div(mod(x - p, NX), 2)
-                first = lax.rem(z_from, NL) * ROWS + p * HALF + k * 32
+                feature = 2 * lax.div(z_from, NL) + lax.div(mod(x - p_here, NX), 2)
+                first = lax.rem(z_from, NL) * ROWS + p_here * HALF + k * 32
                 src = grads.at[feature, pl.ds(pl.multiple_of(first, 32), 32), :]
             go_now(remote(src, src, z2_send.at[j], z_recv.at[j + 4], device(z_=farther)))
         for copy in own_out(j):
             go_now(copy)
 
-    def side_stream(index):
-        return near_x[0] if index == 0 else near_x[1]
-
-    first_x = jnp.where(k == 0, near_x[0], near_x[1])
-    second_x = jnp.where(k == 0, near_x[1], near_x[0])
-    onward = second_x
     across = mod(x + 2, NX)
 
-    def first_out(j):
-        block = piece(first_x, k, j)
-        return [
-            remote(block, block, x_send.at[2, j], x_recv.at[2, j], device(x_=onward)),
-            remote(block, block, sib_send.at[1, j], sib_recv.at[1, j], device(k_=1 - k)),
-        ]
-
-    def second_out(j):
-        block = piece(second_x, k, j)
-        return [remote(block, block, sib_send.at[2, j], sib_recv.at[2, j], device(k_=1 - k))]
+    def side_out(index, j):
+        block = piece(near_x[index], k, j)
+        copies = [remote(block, block, sib_send.at[1 + index, j], sib_recv.at[1 + index, j], device(k_=1 - k))]
+        if j % 2 == index:
+            copies.insert(0, remote(block, block, x_send.at[2, j], x_recv.at[2, j],
+                                    device(x_=near_x[1 - index])))
+        return copies
 
     def across_out(j):
         block = piece(across, k, j)
@@ -205,12 +213,10 @@
         remote(block, block, x_send.at[0, j], x_recv.at[slot, j], device(k_=1 - k)).wait_recv()
 
     def side_event(j):
-        arrived(piece(first_x, k, j), k, j)
-        for copy in first_out(j):
-            go_now(copy)
-        arrived(piece(second_x, k, j), 1 - k, j)
-        for copy in second_out(j):
-            go_now(copy)
+        for index in (j % 2, 1 - j % 2):
+            arrived(piece(near_x[index], k, j), index, j)
+            for copy in side_out(index, j):
+                go_now(copy)
 
     def across_event(j):
         arrived(piece(across, k, j), 2, j)
@@ -226,21 +232,26 @@
 
     @pl.when(is_home)
     def _():
-        p = lax.rem(x + 4 - lax.div(l, 2), 2)
         block = piece(x, k, 0)
-        block[...] = jnp.where(p == 0, go[0:HALF, :], staged[...])
+
+        @pl.when(p_here == 0)
+        def _():
+            block[...] = go[0:HALF, :]
+
+        @pl.when(p_here == 1)
+        def _():
+            remote(block, block, pre_send, pre_recv, device(x_=near_x[1])).wait_recv()
+
         for copy in own_out(0):
             copy.start()
 
     def home_side():
         @pl.when(is_home)
         def _():
-            arrived(piece(first_x, k, 0), k, 0)
-            for copy in first_out(0):
-                copy.start()
-            arrived(piece(second_x, k, 0), 1 - k, 0)
-            for copy in second_out(0):
-                copy.start()
+            for index in range(2):
+                arrived(piece(near_x[index], k, 0), index, 0)
+                for copy in side_out(index, 0):
+                    copy.start()
 
     def home_across():
         @pl.when(is_home)
@@ -257,37 +268,48 @@
     w_event(1, 1)
     own_event(4)
     side_event(1)
-    home_across()
     side_event(2)
     w_event(2, 0)
+    side_event(3)
+    home_across()
+
+    kv_halo = remote(kvx.at[pl.ds(ROWS, ROWS), :], kvx.at[pl.ds(0, ROWS), :],
+                     halo_send.at[0], halo_recv.at[0], along(1))
+
+    @pl.when(l == NL - 1)
+    def _():
+        pl.semaphore_wait(hello_y, 1)
+
+    go_now(kv_halo)
+
+    side_event(4)
+    w_event(2, 1)
     own_event(5)
-    side_event(3)
     across_event(1)
-    w_event(2, 1)
     own_event(6)
-    side_event(4)
     across_event(2)
     own_event(7)
     w_event(3, 0)
-    side_event(5)
     across_event(3)
     own_event(8)
     w_event(3, 1)
+    across_event(4)
+    side_event(5)
     side_event(6)
-    across_event(4)
+    w_arrived(0, 4, 0)
+    w_arrived(1, 4, 1)
     side_event(7)
     across_event(5)
     side_event(8)
-    for j in (6, 7, 8):
-        across_event(j)
-    w_arrived(0, 4, 0)
-    w_arrived(1, 4, 1)
+    across_event(6)
+    across_event(7)
+    across_event(8)
 
     def from_sibling(stream, xs, j):
         block = piece(xs, 1 - k, j)
         remote(block, block, sib_send.at[stream, j], sib_recv.at[stream, j], device(k_=1 - k)).wait_recv()
 
-    streams = ((0, x), (1, second_x), (2, first_x), (3, across))
+    streams = ((0, x), (1, near_x[0]), (2, near_x[1]), (3, across))
     for j in range(1, 9):
         for stream, xs in streams:
             from_sibling(stream, xs, j)
@@ -312,8 +334,7 @@
         go_now(part_copy(i))
     mine = partial(l)
 
-    remote(kvx.at[pl.ds(ROWS, ROWS), :], kvx.at[pl.ds(0, ROWS), :],
-           halo_send.at[0], halo_recv.at[0], along(1)).wait_recv()
+    kv_halo.wait_recv()
     kvx[0:ROWS, :] = jnp.where(ctx > 0, kvx[0:ROWS, :], jnp.zeros((ROWS, WIDE), BF16))
     group_of = lax.div(lax.broadcasted_iota(jnp.int32, (ROWS, WIDE), 1), WIDE // GROUPS)
 
@@ -399,8 +420,12 @@
 
     @pl.when(is_home)
     def _():
-        for copy in own_out(0) + first_out(0) + second_out(0) + across_out(0):
+        for copy in own_out(0) + side_out(0, 0) + side_out(1, 0) + across_out(0):
             copy.wait_send()
+
+    @pl.when(home_half)
+    def _():
+        pre_copy().wait_send()
 
     for i in range(1, NY):
         y_copy(i, mod(y - i, NY)).wait_recv()
@@ -410,10 +435,15 @@
     out_f[...] = final
 
 
+def hand_over(*refs):
+    for src, dst in zip(refs[:4], refs[4:]):
+        dst[...] = src[...]
+
+
 def per_device(*arrays):
     vmem = pl.BlockSpec(memory_space=pltpu.VMEM)
     dma = pltpu.SemaphoreType.DMA
-    return pl.pallas_call(
+    results = pl.pallas_call(
         kernel,
         out_shape=(
             jax.ShapeDtypeStruct((ROWS, WIDE), BF16),
@@ -421,12 +451,18 @@
             jax.ShapeDtypeStruct((ROWS, WIDE), BF16),
             jax.ShapeDtypeStruct((GROUPS, TAPS), F32),
         ),
-        in_specs=[vmem] * 6,
+        in_specs=[pl.BlockSpec(memory_space=pl.ANY)] * 6,
         out_specs=(vmem,) * 4,
         scratch_shapes=[
+            pltpu.VMEM((ROWS, WIDE), BF16),
+            pltpu.VMEM((ROWS, WIDE), BF16),
+            pltpu.VMEM((ROWS, WIDE), BF16),
+            pltpu.VMEM((ROWS, WIDE), BF16),
+            pltpu.VMEM((GROUPS, TAPS), BF16),
+            dma((6,)),
+            pltpu.SemaphoreType.REGULAR,
             pltpu.VMEM((NY, NL * ROWS, WIDE), BF16),
             pltpu.VMEM((NY, WIDE, WIDE), BF16),
-            pltpu.VMEM((HALF, WIDE), BF16),
             pltpu.VMEM((NL - 1, ROWS, WIDE), BF16),
             pltpu.VMEM((NL - 1, ROWS, WIDE), BF16),
             pltpu.VMEM((2 * ROWS, WIDE), BF16),
@@ -445,6 +481,13 @@
         compiler_params=pltpu.CompilerParams(collective_id=0, has_side_effects=True),
         name="block_backward",
     )(*arrays)
+    return pl.pallas_call(
+        hand_over,
+        out_shape=tuple(jax.ShapeDtypeStruct(a.shape, a.dtype) for a in results),
+        in_specs=[vmem] * 4,
+        out_specs=(vmem,) * 4,
+        name="hand_over",
+    )(*results)
 
 
 def solution(mesh):

time: 71.5 us -> 68.1 us (0.952)
  local copies, waits for them, and re-layouts: 3.66 us -> 0 us
    unnamed x10 -> x0, local copies, waits for them, and re-layouts: 3.66 us -> none
    pallas_call x0 -> x1, Pallas kernels: none -> 1.59 us  [per_device(): pl.pallas_call(hand_over, out_shape=tuple((jax.ShapeDtypeStruct(a.shape,...]
    pallas_call x1, Pallas kernels: 66.9 us -> 65.6 us  [per_device(): pl.pallas_call(kernel, out_shape=(jax.ShapeDtypeStruct((ROWS, WIDE), BF16...]
where the time goes in v2:
time: 68.1 us; the launch traced here: 67.8 us
  Pallas kernels  67.2 us (99%)
    pallas_call x1, Pallas kernels, per_device(): pl.pallas_call(kernel, out_shape=(jax.ShapeDtypeStruct((ROWS, WIDE), BF16...  65.6 us
    pallas_call x1, Pallas kernels, per_device(): pl.pallas_call(hand_over, out_shape=tuple((jax.ShapeDtypeStruct(a.shape,...  1.59 us

profile of v2, /device:TPU:1, one launch (start us, length us, event | category | flops | bytes accessed | tf_op | source)
XLA Modules:
  0.0 67.8 jit_solution(4625672550742326342)
XLA Ops:
  0.6 65.6 %block_backward.1 = (bf16[128,256]{1,0:T(8,128)(2,1)}, bf16[128,256]{1,0:T(8,128)(2,1)}, bf16[128,256]{1,0:T(8,128)(2,1)}, f32[16,128]{1,0:T(8,128)}) custom-call(bf16[128,256]{1,0:T(8,128)(2,1)} %go_in.1, bf16[128,256]{1,0:T(8,128)(2,1)} %queries_in.1, bf16[128,256]{1,0:T(8,128)(2,1)} %keys_in.1, bf16[128,256]{1,0:T(8,128)(2,1)} %values_in.1, ...), custom_call_target="tpu_custom_call" | custom-call | tf_op jit(solution)/shard_map/block_backward/pallas_call | solution.py:446
  66.3 1.6 %hand_over.1 = (bf16[128,256]{1,0:T(8,128)(2,1)}, bf16[128,256]{1,0:T(8,128)(2,1)}, bf16[128,256]{1,0:T(8,128)(2,1)}, f32[16,128]{1,0:T(8,128)}) custom-call(bf16[128,256]{1,0:T(8,128)(2,1)} %get-tuple-element.8.refs_0_, bf16[128,256]{1,0:T(8,128)(2,1)} %get-tuple-element.9.refs_1_, bf16[128,256]{1,0:T(8,128)(2,1)} %get-tuple-element.10.refs_2_, ...), custom_call_target="tpu_custom_call" | custom-call | tf_op jit(solution)/shard_map/hand_over/pallas_call | solution.py:484

commit v3 on v2

--- a/solution.py
+++ b/solution.py
@@ -175,9 +175,9 @@
     def own_out(j):
         block = piece(x, k, j)
         return [
-            remote(block, block, sib_send.at[0, j], sib_recv.at[0, j], device(k_=1 - k)),
             remote(block, block, x_send.at[0, j], x_recv.at[0, j], device(x_=near_x[1])),
             remote(block, block, x_send.at[1, j], x_recv.at[1, j], device(x_=near_x[0])),
+            remote(block, block, sib_send.at[0, j], sib_recv.at[0, j], device(k_=1 - k)),
         ]
 
     def own_event(j):
@@ -262,15 +262,18 @@
 
     own_event(1)
     own_event(2)
+    own_event(3)
+    own_event(4)
     w_event(1, 0)
-    own_event(3)
+    w_event(1, 1)
     home_side()
-    w_event(1, 1)
-    own_event(4)
     side_event(1)
     side_event(2)
-    w_event(2, 0)
+    own_event(5)
     side_event(3)
+    own_event(6)
+    side_event(4)
+    own_event(7)
     home_across()
 
     kv_halo = remote(kvx.at[pl.ds(ROWS, ROWS), :], kvx.at[pl.ds(0, ROWS), :],
@@ -282,28 +285,25 @@
 
     go_now(kv_halo)
 
-    side_event(4)
+    own_event(8)
+    w_event(2, 0)
+    across_event(1)
+    across_event(2)
     w_event(2, 1)
-    own_event(5)
-    across_event(1)
-    own_event(6)
-    across_event(2)
-    own_event(7)
-    w_event(3, 0)
     across_event(3)
-    own_event(8)
-    w_event(3, 1)
     across_event(4)
     side_event(5)
     side_event(6)
+    side_event(7)
+    side_event(8)
+    w_event(3, 0)
+    across_event(5)
+    across_event(6)
+    w_event(3, 1)
+    across_event(7)
+    across_event(8)
     w_arrived(0, 4, 0)
     w_arrived(1, 4, 1)
-    side_event(7)
-    across_event(5)
-    side_event(8)
-    across_event(6)
-    across_event(7)
-    across_event(8)
 
     def from_sibling(stream, xs, j):
         block = piece(xs, 1 - k, j)

time: 68.1 us -> 65.3 us (0.959)
  Pallas kernels: 67.2 us -> 64 us
    pallas_call x1, Pallas kernels: 65.6 us -> 62.4 us  [per_device(): pl.pallas_call(kernel, out_shape=(jax.ShapeDtypeStruct((ROWS, WIDE), BF16...]
where the time goes in v3:
time: 65.3 us; the launch traced here: 64.6 us
  Pallas kernels  64 us (98%)
    pallas_call x1, Pallas kernels, per_device(): pl.pallas_call(kernel, out_shape=(jax.ShapeDtypeStruct((ROWS, WIDE), BF16...  62.4 us
    pallas_call x1, Pallas kernels, per_device(): pl.pallas_call(hand_over, out_shape=tuple((jax.ShapeDtypeStruct(a.shape,...  1.59 us

profile of v3, /device:TPU:1, one launch (start us, length us, event | category | flops | bytes accessed | tf_op | source)
XLA Modules:
  0.0 64.6 jit_solution(16512685086707289497)
XLA Ops:
  0.6 62.4 %block_backward.1 = (bf16[128,256]{1,0:T(8,128)(2,1)}, bf16[128,256]{1,0:T(8,128)(2,1)}, bf16[128,256]{1,0:T(8,128)(2,1)}, f32[16,128]{1,0:T(8,128)}) custom-call(bf16[128,256]{1,0:T(8,128)(2,1)} %go_in.1, bf16[128,256]{1,0:T(8,128)(2,1)} %queries_in.1, bf16[128,256]{1,0:T(8,128)(2,1)} %keys_in.1, bf16[128,256]{1,0:T(8,128)(2,1)} %values_in.1, ...), custom_call_target="tpu_custom_call" | custom-call | tf_op jit(solution)/shard_map/block_backward/pallas_call | solution.py:446
  63.0 1.6 %hand_over.1 = (bf16[128,256]{1,0:T(8,128)(2,1)}, bf16[128,256]{1,0:T(8,128)(2,1)}, bf16[128,256]{1,0:T(8,128)(2,1)}, f32[16,128]{1,0:T(8,128)}) custom-call(bf16[128,256]{1,0:T(8,128)(2,1)} %get-tuple-element.8.refs_0_, bf16[128,256]{1,0:T(8,128)(2,1)} %get-tuple-element.9.refs_1_, bf16[128,256]{1,0:T(8,128)(2,1)} %get-tuple-element.10.refs_2_, ...), custom_call_target="tpu_custom_call" | custom-call | tf_op jit(solution)/shard_map/hand_over/pallas_call | solution.py:484

commit v4 on v3

--- a/solution.py
+++ b/solution.py
@@ -446,10 +446,10 @@
     results = pl.pallas_call(
         kernel,
         out_shape=(
-            jax.ShapeDtypeStruct((ROWS, WIDE), BF16),
-            jax.ShapeDtypeStruct((ROWS, WIDE), BF16),
-            jax.ShapeDtypeStruct((ROWS, WIDE), BF16),
-            jax.ShapeDtypeStruct((GROUPS, TAPS), F32),
+            pltpu.VMEM((ROWS, WIDE), BF16),
+            pltpu.VMEM((ROWS, WIDE), BF16),
+            pltpu.VMEM((ROWS, WIDE), BF16),
+            pltpu.VMEM((GROUPS, TAPS), F32),
         ),
         in_specs=[pl.BlockSpec(memory_space=pl.ANY)] * 6,
         out_specs=(vmem,) * 4,
@@ -487,7 +487,7 @@
         in_specs=[vmem] * 4,
         out_specs=(vmem,) * 4,
         name="hand_over",
-    )(*results)
+    )(*[pltpu.with_memory_space_constraint(r, pltpu.VMEM) for r in results])
 
 
 def solution(mesh):

time: 65.3 us -> 63.7 us (0.975)
  Pallas kernels: 64 us -> 62.4 us
    pallas_call x1, Pallas kernels: 1.59 us -> 0.69 us  [per_device(): pl.pallas_call(hand_over, out_shape=tuple((jax.ShapeDtypeStruct(a.shape,...]
    pallas_call x1, Pallas kernels: 62.4 us -> 61.7 us  [per_device(): pl.pallas_call(kernel, out_shape=(pltpu.VMEM((ROWS, WIDE), BF16), pltpu.V...]
where the time goes in v4:
time: 63.7 us; the launch traced here: 63.1 us
  Pallas kernels  62.4 us (98%)
  between operations  0.64 us (1%)
    pallas_call x1, Pallas kernels, per_device(): pl.pallas_call(kernel, out_shape=(pltpu.VMEM((ROWS, WIDE), BF16), pltpu.V...  61.7 us

profile of v4, /device:TPU:1, one launch (start us, length us, event | category | flops | bytes accessed | tf_op | source)
XLA Modules:
  0.0 63.1 jit_solution(8474770229031465662)
XLA Ops:
  0.6 61.7 %block_backward.1 = (bf16[128,256]{1,0:T(8,128)(2,1)S(1)}, bf16[128,256]{1,0:T(8,128)(2,1)S(1)}, bf16[128,256]{1,0:T(8,128)(2,1)S(1)}, f32[16,128]{1,0:T(8,128)S(1)}) custom-call(bf16[128,256]{1,0:T(8,128)(2,1)} %go_in.1, bf16[128,256]{1,0:T(8,128)(2,1)} %queries_in.1, bf16[128,256]{1,0:T(8,128)(2,1)} %keys_in.1, bf16[128,256]{1,0:T(8,128)(2,1)} %values_in.1, ...), custom_call_target="tpu_custom_call" | custom-call | tf_op jit(solution)/shard_map/block_backward/pallas_call | solution.py:446
  62.4 0.7 %hand_over.1 = (bf16[128,256]{1,0:T(8,128)(2,1)}, bf16[128,256]{1,0:T(8,128)(2,1)}, bf16[128,256]{1,0:T(8,128)(2,1)}, f32[16,128]{1,0:T(8,128)}) custom-call(bf16[128,256]{1,0:T(8,128)(2,1)S(1)} %get-tuple-element.8.refs_0_, bf16[128,256]{1,0:T(8,128)(2,1)S(1)} %get-tuple-element.9.refs_1_, bf16[128,256]{1,0:T(8,128)(2,1)S(1)} %get-tuple-element.10.refs_2_, ...), custom_call_target="tpu_custom_call" | custom-call | tf_op jit(solution)/shard_map/hand_over/pallas_call | solution.py:484
